TPU v7x, 1024 devices: a whole 4x8x16 slice. The times are simulated.
1024 devices in a mesh: pitch: 64 (over z_hi, y, core), span: 16 (over z_lo, x).
Axes of the slice: x: 4, y: 8, z: 16 (z_hi: 4, z_lo: 4; z = z_hi * 4 + z_lo), core: 2. Of those that a mesh axis runs over, the one named last changes fastest.
Arguments:
- state: float32 [5, 5, 5, 5, 128, 16, 128], P(None, None, None, None, 'pitch', 'span'), may hold values from -6 to 6
- wake_planes: float32 [5, 5, 5, 128, 16], P(None, None, None, 'pitch', 'span'), may hold values from -6 to 6
- bar_offsets: int32 [3], replicated, may hold values from 0 to 1, as said below
Outputs:
- advanced: float32 [5, 5, 5, 5, 128, 16, 128], P(None, None, None, None, 'pitch', 'span')
Inputs may be any that keep to these rules, and one draw needn't show every extreme that they name: `bar_offsets`: some section has offset 1 and some section offset 0.
All inputs are finite; a program needn't handle non-finite values.
Results may differ from a plain program's by a relative error of at most 0.0001.
Values sent between devices are 32-bit elements; how exact they have to be, the bound alone decides.
A program may use at most 64 MiB of HBM per device.

v0:
```python
import functools

import jax
import jax.numpy as jnp
import numpy as np
from jax import lax
from jax.experimental import pallas as pl
from jax.experimental.pallas import tpu as pltpu
from jax.sharding import PartitionSpec as P

MEAN = (0.5, 0.3, 0.0)
SPEED = (1.5, 1.3, 1.0)
SIZE = (1.0, 0.8, 1.2)
END = 0.1
DT = 0.01
STAGES = ((0.0, 1.0), (0.75, 0.25), (1.0 / 3.0, 2.0 / 3.0))
MESH = pl.DeviceIdType.MESH
F32 = jnp.float32
VS, AS, PS, SS = 250, 50, 10, 2
ROWS = 1256


def derivative_matrix():
    x = np.array([-1.0, -np.sqrt(3.0 / 7.0), 0.0, np.sqrt(3.0 / 7.0), 1.0])
    c = np.array([np.prod([x[j] - x[k] for k in range(5) if k != j]) for j in range(5)])
    d = np.zeros((5, 5))
    for i in range(5):
        for j in range(5):
            if i != j:
                d[i, j] = c[i] / (c[j] * (x[i] - x[j]))
        d[i, i] = sum(1.0 / (x[i] - x[k]) for k in range(5) if k != i)
    d[4, 4] -= 0.5 / END
    d[0, 0] += 0.5 / END
    return d


MATRIX = derivative_matrix()


def derive(f, scale):
    d = MATRIX * scale
    s0, m0, s1, m1 = f[0] + f[4], f[0] - f[4], f[1] + f[3], f[1] - f[3]
    out = [None] * 5
    for i in range(2):
        odd = (
            float((d[i, 0] + d[i, 4]) / 2) * s0
            + float((d[i, 1] + d[i, 3]) / 2) * s1
            + float(d[i, 2]) * f[2]
        )
        even = float((d[i, 0] - d[i, 4]) / 2) * m0 + float((d[i, 1] - d[i, 3]) / 2) * m1
        out[i] = even + odd
        out[4 - i] = even - odd
    out[2] = float(d[2, 0]) * m0 + float(d[2, 1]) * m1
    return out


def others(direction):
    return [v for v in (1, 2, 3) if v != 1 + direction]


def minus_part(v, direction, h):
    o1, o2 = others(direction)
    n = v[1 + direction]
    return [h * (v[0] - n), h * (n - v[4]), h * v[o1], h * v[o2]]


def plus_part(v, direction, h):
    o1, o2 = others(direction)
    n, g = v[1 + direction], h * (SPEED[direction] + MEAN[direction])
    if direction == 2:
        both = h * (v[0] + n)
        return [both, h * (n + v[4]), h * v[o1], h * v[o2]]
    return [g * v[0] + h * n, g * n + h * v[4], g * v[o1], g * v[o2], g * v[4] + h * n]


def spread(parts, direction, upper):
    o1, o2 = others(direction)
    out = [None] * 5
    out[0], out[1 + direction], out[o1], out[o2] = parts[:4]
    if upper:
        out[4] = -parts[1]
    elif direction == 2:
        out[4] = parts[1]
    else:
        out[4] = parts[4]
    return out


class Stage:
    def __init__(self, index):
        self.alpha, self.beta = STAGES[index]
        self.bdt = self.beta * DT
        self.k = [-self.bdt * 2.0 / h for h in SIZE]
        self.h = [0.5 * self.bdt * 2.0 / (h * END) for h in SIZE]


def axial_pass(st, v_ref, s_ref, w_ref):
    lane = lax.broadcasted_iota(jnp.int32, (8, 128), 1)
    first, last = lane == 0, lane == 127
    h, k, u = st.h[0], st.k[0], MEAN[0]

    @pl.loop(0, 7)
    def _(i):
        r0 = jnp.minimum(8 * i, 42)
        rows = lambda v, a: pl.ds(v * VS + a * AS + r0, 8)
        f = [[v_ref[rows(v, a), :] for a in range(5)] for v in range(5)]
        g = [
            derive([u * f[0][a] + f[1][a] for a in range(5)], k),
            derive([u * f[1][a] + f[4][a] for a in range(5)], k),
            derive(f[2], k * u),
            derive(f[3], k * u),
            derive([u * f[4][a] + f[1][a] for a in range(5)], k),
        ]
        lo, up = [f[v][0] for v in range(5)], [f[v][4] for v in range(5)]
        mine = minus_part(up, 0, h)
        nxt = [
            jnp.where(last, own, pltpu.roll(q, 127, 1))
            for q, own in zip(minus_part(lo, 0, h), mine)
        ]
        prv = [jnp.where(first, 0.0, pltpu.roll(q, 1, 1)) for q in plus_part(up, 0, h)]
        nxt, prv = spread(nxt, 0, True), spread(prv, 0, False)
        for v in range(5):
            for a in range(5):
                diag = st.beta - (h * SPEED[0] if a in (0, 4) else 0.0)
                acc = diag * f[v][a] + g[v][a]
                if st.alpha:
                    acc = acc + st.alpha * s_ref[rows(v, a), :]
                if a == 0:
                    acc = acc + prv[v]
                if a == 4:
                    acc = acc + nxt[v]
                w_ref[rows(v, a), :] = acc


def pitch_pass(st, v_ref, w_ref):
    h, k, u = st.h[1], st.k[1], MEAN[1]
    for r0, n in ((0, 8), (8, 2)):
        even = lax.broadcasted_iota(jnp.int32, (n, 128), 0) % 2 == 0

        @pl.loop(0, 5)
        def _(a):
            rows = lambda v, p, off=0: pl.ds(v * VS + a * AS + p * PS + r0 + off, n)
            f = [[v_ref[rows(v, p), :] for p in range(5)] for v in range(5)]
            g = [
                derive([u * f[0][p] + f[2][p] for p in range(5)], k),
                derive(f[1], k * u),
                derive([u * f[2][p] + f[4][p] for p in range(5)], k),
                derive(f[3], k * u),
                derive([u * f[4][p] + f[2][p] for p in range(5)], k),
            ]
            lo = [v_ref[rows(v, 0, 1), :] for v in range(5)]
            up = [v_ref[rows(v, 4, -1), :] for v in range(5)]
            nxt = spread([jnp.where(even, q, 0.0) for q in minus_part(lo, 1, h)], 1, True)
            prv = spread([jnp.where(even, 0.0, q) for q in plus_part(up, 1, h)], 1, False)
            for v in range(5):
                for p in range(5):
                    acc = w_ref[rows(v, p), :] + g[v][p]
                    if p == 0:
                        acc = acc + prv[v] - (h * SPEED[1]) * f[v][0]
                    if p == 4:
                        acc = acc + nxt[v] - (h * SPEED[1]) * f[v][4]
                    w_ref[rows(v, p), :] = acc


def span_rows(v, s, k):
    return pl.ds(v * VS + s * SS + k, 25, PS)


def span_pass(st, v_ref, w_ref):
    h, k = st.h[2], st.k[2]
    for c in range(2):
        un = [v_ref[span_rows(3, s, c), :] for s in range(5)]
        pr = [v_ref[span_rows(4, s, c), :] for s in range(5)]
        g, gp = derive(un, k), derive(pr, k)
        for s in range(5):
            for v in range(5):
                acc = w_ref[span_rows(v, s, c), :]
                if v in (0, 4):
                    acc = acc + g[s]
                if v == 3:
                    acc = acc + gp[s]
                if s in (0, 4):
                    own = un[s] if v == 3 else pr[s] if v == 4 else v_ref[span_rows(v, s, c), :]
                    acc = acc - (h * SPEED[2]) * own
                elif v in (1, 2):
                    continue
                w_ref[span_rows(v, s, c), :] = acc


def span_message(st, v_ref, down_ref, up_ref):
    for c in range(2):
        lo = [v_ref[span_rows(v, 0, c), :] for v in range(5)]
        up = [v_ref[span_rows(v, 4, c), :] for v in range(5)]
        for j, q in enumerate(minus_part(lo, 2, st.h[2])):
            down_ref[pl.ds((2 * j + c) * 25, 25), :] = q
        for j, q in enumerate(plus_part(up, 2, st.h[2])):
            up_ref[pl.ds((2 * j + c) * 25, 25), :] = q


def span_apply(w_ref, msg_ref, upper):
    s = 4 if upper else 0
    for c in range(2):
        parts = [msg_ref[pl.ds((2 * j + c) * 25, 25), :] for j in range(4)]
        for v, q in enumerate(spread(parts, 2, upper)):
            w_ref[span_rows(v, s, c), :] = w_ref[span_rows(v, s, c), :] + q


def pitch_rows(v, a, p, c):
    return pl.ds(v * VS + a * AS + p * PS + c, 5, SS)


def pitch_message(st, v_ref, down_ref, up_ref):
    @pl.loop(0, 5)
    def _(a):
        lo = [v_ref[pitch_rows(v, a, 0, 0), :] for v in range(5)]
        up = [v_ref[pitch_rows(v, a, 4, 1), :] for v in range(5)]
        for j, q in enumerate(minus_part(lo, 1, st.h[1])):
            down_ref[pl.ds(j * 25 + a * 5, 5), :] = q
        for j, q in enumerate(plus_part(up, 1, st.h[1])):
            up_ref[pl.ds(j * 25 + a * 5, 5), :] = q


def pitch_apply(w_ref, msg_ref, upper):
    p, c, n = (4, 1, 4) if upper else (0, 0, 5)

    @pl.loop(0, 5)
    def _(a):
        parts = [msg_ref[pl.ds(j * 25 + a * 5, 5), :] for j in range(n)]
        for v, q in enumerate(spread(parts, 1, upper)):
            w_ref[pitch_rows(v, a, p, c), :] = w_ref[pitch_rows(v, a, p, c), :] + q


def pack_wake(wake_ref, tmp_ref, out_ref):
    lane = lax.broadcasted_iota(jnp.int32, (2, 128), 1)
    total = jnp.zeros((2, 128), F32)
    for i in range(25):
        tmp_ref[i, :, 0:5] = wake_ref[i]
    for i in range(25):
        tile = jnp.where(lane < 5, tmp_ref[i], 0.0)
        total = total + (pltpu.roll(tile, 5 * i, 1) if i else tile)
    out_ref[...] = total


def wake_apply(st, w_ref, wake_ref, offset):
    row = lax.broadcasted_iota(jnp.int32, (50, 128), 0)
    lane = lax.broadcasted_iota(jnp.int32, (50, 128), 1)
    flip = (row + offset) % 2 == 0
    tile = wake_ref[...]
    chosen = jnp.where(
        flip, jnp.broadcast_to(tile[0:1], (50, 128)), jnp.broadcast_to(tile[1:2], (50, 128))
    )
    g = []
    for v in range(5):
        picked = jnp.where(lane == v * 25 + row // 2, chosen, 0.0)
        g.append(jnp.broadcast_to(jnp.sum(picked, axis=1, keepdims=True), (50, 128)))
    parts = spread(plus_part(g, 0, st.h[0]), 0, False)
    for v in range(5):
        rows = pl.ds(v * VS, 50)
        w_ref[rows, :] = w_ref[rows, :] + jnp.where(lane == 0, parts[v], 0.0)


def kernel(
    np_, ns_, offs_ref, state_hbm, wake_ref, out_hbm,
    s_ref, w1_ref, w2_ref, w3_ref, tmp_ref, own_wake, got_wake,
    p_down, p_up, s_down, s_up, r_next, r_prev, t_next, t_prev,
    send_sem, recv_sem, wake_send, wake_recv, io_sem,
):
    ip, js = lax.axis_index("pitch"), lax.axis_index("span")
    p_next, p_prev = lax.rem(ip + 1, np_), lax.rem(ip + np_ - 1, np_)
    has_next, has_prev = js < ns_ - 1, js > 0
    load = pltpu.make_async_copy(
        state_hbm.reshape(1250, 128), s_ref.at[pl.ds(0, 1250)], io_sem.at[0]
    )
    load.start()

    barrier = pltpu.get_barrier_semaphore()
    for q in (p_next, p_prev):
        pl.semaphore_signal(barrier, inc=1, device_id={"pitch": q}, device_id_type=MESH)

    @pl.when(has_next)
    def _():
        pl.semaphore_signal(barrier, inc=1, device_id={"span": js + 1}, device_id_type=MESH)

    @pl.when(has_prev)
    def _():
        pl.semaphore_signal(barrier, inc=1, device_id={"span": js - 1}, device_id_type=MESH)

    pack_wake(wake_ref, tmp_ref, own_wake)
    load.wait()
    pl.semaphore_wait(
        barrier, 2 + has_next.astype(jnp.int32) + has_prev.astype(jnp.int32)
    )

    def remote(src, dst, n, way, device):
        return pltpu.make_async_remote_copy(
            src_ref=src, dst_ref=dst, send_sem=send_sem.at[n, way], recv_sem=recv_sem.at[n, way],
            device_id=device, device_id_type=MESH,
        )

    def wake_copy(n):
        return pltpu.make_async_remote_copy(
            src_ref=own_wake if n == 0 else got_wake.at[n - 1], dst_ref=got_wake.at[n],
            send_sem=wake_send.at[n], recv_sem=wake_recv.at[n],
            device_id={"pitch": p_next}, device_id_type=MESH,
        )

    values = [s_ref, w1_ref, w2_ref, w3_ref]
    wake_copy(0).start()
    copies = []
    for n in range(3):
        st, v_ref, w_ref = Stage(n), values[n], values[n + 1]
        to_next = remote(p_up.at[n], r_prev.at[n], n, 0, {"pitch": p_next})
        to_prev = remote(p_down.at[n], r_next.at[n], n, 1, {"pitch": p_prev})
        to_above = remote(s_up.at[n], t_prev.at[n], n, 2, {"span": js + 1})
        to_below = remote(s_down.at[n], t_next.at[n], n, 3, {"span": js - 1})
        pitch_message(st, v_ref, p_down.at[n], p_up.at[n])
        to_next.start()
        to_prev.start()
        span_message(st, v_ref, s_down.at[n], s_up.at[n])
        pl.when(has_next)(to_above.start)
        pl.when(has_prev)(to_below.start)

        axial_pass(st, v_ref, s_ref, w_ref)
        pitch_pass(st, v_ref, w_ref)
        span_pass(st, v_ref, w_ref)
        wake_copy(n).wait_recv()
        if n < 2:
            wake_copy(n + 1).start()
        wake_apply(st, w_ref, got_wake.at[n], offs_ref[n])

        @pl.when(has_prev)
        def _():
            to_above.wait_recv()
            span_apply(w_ref, t_prev.at[n], False)

        @pl.when(has_next)
        def _():
            to_below.wait_recv()
            span_apply(w_ref, t_next.at[n], True)

        to_next.wait_recv()
        pitch_apply(w_ref, r_prev.at[n], False)
        to_prev.wait_recv()
        pitch_apply(w_ref, r_next.at[n], True)
        copies.append((to_next, to_prev, to_above, to_below))

    store = pltpu.make_async_copy(
        w3_ref.at[pl.ds(0, 1250)], out_hbm.reshape(1250, 128), io_sem.at[1]
    )
    store.start()
    for n, (to_next, to_prev, to_above, to_below) in enumerate(copies):
        wake_copy(n).wait_send()
        to_next.wait_send()
        to_prev.wait_send()
        pl.when(has_next)(to_above.wait_send)
        pl.when(has_prev)(to_below.wait_send)
    store.wait()


def solution(mesh):
    np_, ns_ = mesh.shape["pitch"], mesh.shape["span"]

    def step(state, wake, offsets):
        flat = state.reshape(625, 2, 128)
        rows = jnp.transpose(wake, (0, 1, 3, 4, 2)).reshape(25, 2, 5)
        out = pl.pallas_call(
            functools.partial(kernel, np_, ns_),
            out_shape=jax.ShapeDtypeStruct((625, 2, 128), F32),
            in_specs=[
                pl.BlockSpec(memory_space=pltpu.SMEM),
                pl.BlockSpec(memory_space=pl.ANY),
                pl.BlockSpec(memory_space=pltpu.VMEM),
            ],
            out_specs=pl.BlockSpec(memory_space=pl.ANY),
            scratch_shapes=[pltpu.VMEM((ROWS, 128), F32)] * 4
            + [
                pltpu.VMEM((25, 2, 128), F32),
                pltpu.VMEM((2, 128), F32),
                pltpu.VMEM((3, 2, 128), F32),
                pltpu.VMEM((3, 100, 128), F32),
                pltpu.VMEM((3, 125, 128), F32),
                pltpu.VMEM((3, 200, 128), F32),
                pltpu.VMEM((3, 200, 128), F32),
                pltpu.VMEM((3, 100, 128), F32),
                pltpu.VMEM((3, 125, 128), F32),
                pltpu.VMEM((3, 200, 128), F32),
                pltpu.VMEM((3, 200, 128), F32),
                pltpu.SemaphoreType.DMA((3, 4)),
                pltpu.SemaphoreType.DMA((3, 4)),
                pltpu.SemaphoreType.DMA((3,)),
                pltpu.SemaphoreType.DMA((3,)),
                pltpu.SemaphoreType.DMA((2,)),
            ],
            compiler_params=pltpu.CompilerParams(collective_id=0, has_side_effects=True),
        )(offsets, flat, rows)
        return out.reshape(state.shape)

    spec = P(None, None, None, None, "pitch", "span", None)
    return jax.shard_map(
        step,
        mesh=mesh,
        in_specs=(spec, P(None, None, None, "pitch", "span"), P()),
        out_specs=spec,
        check_vma=False,
    )
```

profile of v0, /device:TPU:6, one launch (start us, length us, event | category | flops | bytes accessed | tf_op | source)
XLA Modules:
  0.0 42.7 jit_solution(16162587519399122358)
XLA Ops:
  0.0 40.4 %shard_map.37 = f32[625,2,128]{2,1,0:T(2,128)} custom-call(s32[3]{0:T(128)} %offs_ref.1, f32[625,2,128]{2,1,0:T(2,128)} %bitcast.8, f32[25,2,5]{2,1,0:T(2,128)} %bitcast.9), custom_call_target="tpu_custom_call" | custom-call | tf_op jit(solution)/shard_map/pallas_call | solution.py:366
  40.4 2.4 %copy.6 = f32[5,5,5,5,2,1,128]{6,5,4,3,2,1,0:T(1,128)} copy(f32[5,5,5,5,2,1,128]{6,5,4,3,2,1,0:T(1,128)} %bitcast.7) | data formatting | bytes 1280000
where the time goes:
time: 43 us; the launch traced here: 42.7 us
  Pallas kernels  40.4 us (94%)
  local copies, waits for them, and re-layouts  2.35 us (5%)
    pallas_call x1, Pallas kernels, step(): pl.pallas_call(functools.partial(kernel, np_, ns_), out_shape=jax.ShapeDt...  40.4 us
    unnamed x1, local copies, waits for them, and re-layouts  2.35 us

commit v1 on v0

--- a/solution.py
+++ b/solution.py
@@ -17,7 +17,8 @@
 MESH = pl.DeviceIdType.MESH
 F32 = jnp.float32
 VS, AS, PS, SS = 250, 50, 10, 2
-ROWS = 1256
+ROWS = 1408
+FAR = 16
 
 
 def derivative_matrix():
@@ -87,8 +88,10 @@
 
 
 class Stage:
-    def __init__(self, index):
+    def __init__(self, index, carry=True):
         self.alpha, self.beta = STAGES[index]
+        if not carry:
+            self.alpha = 0.0
         self.bdt = self.beta * DT
         self.k = [-self.bdt * 2.0 / h for h in SIZE]
         self.h = [0.5 * self.bdt * 2.0 / (h * END) for h in SIZE]
@@ -259,11 +262,52 @@
         w_ref[rows, :] = w_ref[rows, :] + jnp.where(lane == 0, parts[v], 0.0)
 
 
+EDGES = ((0, 0), (4, 1))
+
+
+def edge_rows(v, s, i):
+    p, c = EDGES[i]
+    return pl.ds(v * VS + p * PS + s * SS + c, 5, AS)
+
+
+def edge_message(st, v_ref, down_ref, up_ref):
+    for i in range(2):
+        lo = [v_ref[edge_rows(v, 0, i), :] for v in range(5)]
+        up = [v_ref[edge_rows(v, 4, i), :] for v in range(5)]
+        for j, q in enumerate(minus_part(lo, 2, st.h[2])):
+            down_ref[pl.ds((2 * j + i) * 5, 5), :] = q
+        for j, q in enumerate(plus_part(up, 2, st.h[2])):
+            up_ref[pl.ds((2 * j + i) * 5, 5), :] = q
+
+
+def edge_apply(w_ref, msg_ref, upper):
+    s = 4 if upper else 0
+    for i in range(2):
+        parts = [msg_ref[pl.ds((2 * j + i) * 5, 5), :] for j in range(4)]
+        for v, q in enumerate(spread(parts, 2, upper)):
+            w_ref[edge_rows(v, s, i), :] = w_ref[edge_rows(v, s, i), :] + q
+
+
+def volume(st, v_ref, s_ref, w_ref):
+    axial_pass(st, v_ref, s_ref, w_ref)
+    pitch_pass(st, v_ref, w_ref)
+    span_pass(st, v_ref, w_ref)
+
+
+def add_rows(a_ref, b_ref, w_ref):
+    @pl.loop(0, 157)
+    def _(i):
+        rows = pl.ds(pl.multiple_of(8 * i, 8), 8)
+        w_ref[rows, :] = a_ref[rows, :] + b_ref[rows, :]
+
+
 def kernel(
-    np_, ns_, offs_ref, state_hbm, wake_ref, out_hbm,
-    s_ref, w1_ref, w2_ref, w3_ref, tmp_ref, own_wake, got_wake,
+    np_, ns_, offs_ref, state_hbm, wake_ref, t3_ref,
+    s_ref, w1_ref, w2_ref, x1_ref, x2_ref, c1_ref, c2_ref, t_ref,
+    tmp_ref, own_wake, got_wake,
     p_down, p_up, s_down, s_up, r_next, r_prev, t_next, t_prev,
-    send_sem, recv_sem, wake_send, wake_recv, io_sem,
+    l_down, l_up, e_down, e_up, e_next, e_prev,
+    send_sem, recv_sem, edge_send, edge_recv, wake_send, wake_recv, io_sem,
 ):
     ip, js = lax.axis_index("pitch"), lax.axis_index("span")
     p_next, p_prev = lax.rem(ip + 1, np_), lax.rem(ip + np_ - 1, np_)
@@ -286,75 +330,149 @@
         pl.semaphore_signal(barrier, inc=1, device_id={"span": js - 1}, device_id_type=MESH)
 
     pack_wake(wake_ref, tmp_ref, own_wake)
-    load.wait()
     pl.semaphore_wait(
         barrier, 2 + has_next.astype(jnp.int32) + has_prev.astype(jnp.int32)
     )
 
-    def remote(src, dst, n, way, device):
+    def remote(src, dst, sends, recvs, device):
         return pltpu.make_async_remote_copy(
-            src_ref=src, dst_ref=dst, send_sem=send_sem.at[n, way], recv_sem=recv_sem.at[n, way],
+            src_ref=src, dst_ref=dst, send_sem=sends, recv_sem=recvs,
             device_id=device, device_id_type=MESH,
         )
 
     def wake_copy(n):
-        return pltpu.make_async_remote_copy(
-            src_ref=own_wake if n == 0 else got_wake.at[n - 1], dst_ref=got_wake.at[n],
-            send_sem=wake_send.at[n], recv_sem=wake_recv.at[n],
-            device_id={"pitch": p_next}, device_id_type=MESH,
+        return remote(
+            own_wake if n == 0 else got_wake.at[n - 1], got_wake.at[n],
+            wake_send.at[n], wake_recv.at[n], {"pitch": p_next},
         )
 
-    values = [s_ref, w1_ref, w2_ref, w3_ref]
-    wake_copy(0).start()
-    copies = []
-    for n in range(3):
-        st, v_ref, w_ref = Stage(n), values[n], values[n + 1]
-        to_next = remote(p_up.at[n], r_prev.at[n], n, 0, {"pitch": p_next})
-        to_prev = remote(p_down.at[n], r_next.at[n], n, 1, {"pitch": p_prev})
-        to_above = remote(s_up.at[n], t_prev.at[n], n, 2, {"span": js + 1})
-        to_below = remote(s_down.at[n], t_next.at[n], n, 3, {"span": js - 1})
-        pitch_message(st, v_ref, p_down.at[n], p_up.at[n])
-        to_next.start()
-        to_prev.start()
-        span_message(st, v_ref, s_down.at[n], s_up.at[n])
-        pl.when(has_next)(to_above.start)
-        pl.when(has_prev)(to_below.start)
-
-        axial_pass(st, v_ref, s_ref, w_ref)
-        pitch_pass(st, v_ref, w_ref)
-        span_pass(st, v_ref, w_ref)
-        wake_copy(n).wait_recv()
-        if n < 2:
-            wake_copy(n + 1).start()
-        wake_apply(st, w_ref, got_wake.at[n], offs_ref[n])
-
+    def pitch_copies(n):
+        return (
+            remote(p_up.at[n, pl.ds(0, 125)], r_prev.at[n, pl.ds(0, 125)], send_sem.at[n, 0], recv_sem.at[n, 0], {"pitch": p_next}),
+            remote(p_down.at[n, pl.ds(0, 100)], r_next.at[n, pl.ds(0, 100)], send_sem.at[n, 1], recv_sem.at[n, 1], {"pitch": p_prev}),
+        )
+
+    def span_copies(n):
+        return (
+            remote(s_up.at[n, pl.ds(0, 200)], t_prev.at[n, pl.ds(0, 200)], send_sem.at[n, 2], recv_sem.at[n, 2], {"span": js + 1}),
+            remote(s_down.at[n, pl.ds(0, 200)], t_next.at[n, pl.ds(0, 200)], send_sem.at[n, 3], recv_sem.at[n, 3], {"span": js - 1}),
+        )
+
+    def edge_copies(n):
+        return (
+            remote(e_up.at[n, pl.ds(0, 40)], e_prev.at[n, pl.ds(0, 40)], edge_send.at[n, 0], edge_recv.at[n, 0], {"span": js + 1}),
+            remote(e_down.at[n, pl.ds(0, 40)], e_next.at[n, pl.ds(0, 40)], edge_send.at[n, 1], edge_recv.at[n, 1], {"span": js - 1}),
+        )
+
+    def span_start(above, below):
+        pl.when(has_next)(above.start)
+        pl.when(has_prev)(below.start)
+
+    def span_receive(above, below, apply, w_ref, prev_ref, next_ref):
         @pl.when(has_prev)
         def _():
-            to_above.wait_recv()
-            span_apply(w_ref, t_prev.at[n], False)
+            above.wait_recv()
+            apply(w_ref, prev_ref, False)
 
         @pl.when(has_next)
         def _():
-            to_below.wait_recv()
-            span_apply(w_ref, t_next.at[n], True)
-
-        to_next.wait_recv()
-        pitch_apply(w_ref, r_prev.at[n], False)
-        to_prev.wait_recv()
-        pitch_apply(w_ref, r_next.at[n], True)
-        copies.append((to_next, to_prev, to_above, to_below))
-
-    store = pltpu.make_async_copy(
-        w3_ref.at[pl.ds(0, 1250)], out_hbm.reshape(1250, 128), io_sem.at[1]
-    )
-    store.start()
-    for n, (to_next, to_prev, to_above, to_below) in enumerate(copies):
+            below.wait_recv()
+            apply(w_ref, next_ref, True)
+
+    pitch, span = [pitch_copies(n) for n in range(3)], [span_copies(n) for n in range(3)]
+    edges = [edge_copies(n) for n in range(2)]
+
+    wake_copy(0).start()
+    stages = [Stage(n) for n in range(3)]
+    linear = Stage(1, carry=False)
+    load.wait()
+    pitch_message(stages[0], s_ref, p_down.at[0], p_up.at[0])
+    for copy in pitch[0]:
+        copy.start()
+    span_message(stages[0], s_ref, s_down.at[0], s_up.at[0])
+    span_start(*span[0])
+    x1_ref[...] = jnp.zeros((ROWS, 128), F32)
+    c1_ref[...] = jnp.zeros((ROWS, 128), F32)
+    pitch_apply(x1_ref, p_down.at[0], True)
+    pitch_apply(x1_ref, p_up.at[0], False)
+    edge_message(linear, x1_ref, e_down.at[0], e_up.at[0])
+    span_start(*edges[0])
+
+    volume(stages[0], s_ref, s_ref, w1_ref)
+    volume(linear, x1_ref, s_ref, x2_ref)
+    wake_copy(0).wait_recv()
+    wake_copy(1).start()
+    wake_apply(stages[0], w1_ref, got_wake.at[0], offs_ref[0])
+    span_receive(*span[0], span_apply, w1_ref, t_prev.at[0], t_next.at[0])
+    span_message(stages[1], w1_ref, s_down.at[1], s_up.at[1])
+    span_start(*span[1])
+    pitch_message(stages[1], w1_ref, p_down.at[1], p_up.at[1])
+    for copy in pitch[1]:
+        copy.start()
+    volume(stages[1], w1_ref, s_ref, w2_ref)
+    wake_copy(1).wait_recv()
+    wake_copy(2).start()
+    wake_apply(stages[1], w2_ref, got_wake.at[1], offs_ref[1])
+
+    def finish_second():
+        span_receive(*span[1], span_apply, w2_ref, t_prev.at[1], t_next.at[1])
+        pitch_message(stages[2], w2_ref, p_down.at[2], p_up.at[2])
+        for copy in pitch[2]:
+            copy.start()
+
+    far = lax.rem(ip, FAR) == FAR - 1
+    pl.when(far)(finish_second)
+
+    pitch[0][0].wait_recv()
+    pitch_apply(c1_ref, r_prev.at[0], False)
+    pitch[0][1].wait_recv()
+    pitch_apply(c1_ref, r_next.at[0], True)
+    edge_message(linear, c1_ref, e_down.at[1], e_up.at[1])
+    span_start(*edges[1])
+    add_rows(w1_ref, c1_ref, t_ref)
+    span_receive(*edges[0], edge_apply, x2_ref, e_prev.at[0], e_next.at[0])
+    pitch_message(stages[1], t_ref, l_down, l_up)
+    pitch_apply(x2_ref, l_down, True)
+    pitch_apply(x2_ref, l_up, False)
+    volume(linear, c1_ref, s_ref, c2_ref)
+    pitch_message(stages[1], x1_ref, l_down, l_up)
+    pitch_apply(c2_ref, l_down, True)
+    pitch_apply(c2_ref, l_up, False)
+    pl.when(jnp.logical_not(far))(finish_second)
+    span_receive(*edges[1], edge_apply, c2_ref, e_prev.at[1], e_next.at[1])
+    pitch[1][0].wait_recv()
+    pitch_apply(c2_ref, r_prev.at[1], False)
+    pitch[1][1].wait_recv()
+    pitch_apply(c2_ref, r_next.at[1], True)
+    add_rows(w2_ref, c2_ref, t_ref)
+
+    span_message(stages[2], t_ref, s_down.at[2], s_up.at[2])
+    span_start(*span[2])
+    volume(stages[2], t_ref, s_ref, t3_ref)
+    wake_copy(2).wait_recv()
+    wake_apply(stages[2], t3_ref, got_wake.at[2], offs_ref[2])
+    pitch_message(stages[2], x2_ref, l_down, l_up)
+    pitch_apply(t3_ref, l_down, True)
+    pitch_apply(t3_ref, l_up, False)
+    span_receive(*span[2], span_apply, t3_ref, t_prev.at[2], t_next.at[2])
+    pitch[2][0].wait_recv()
+    pitch_apply(t3_ref, r_prev.at[2], False)
+    pitch[2][1].wait_recv()
+    pitch_apply(t3_ref, r_next.at[2], True)
+
+    for n in range(3):
         wake_copy(n).wait_send()
-        to_next.wait_send()
-        to_prev.wait_send()
-        pl.when(has_next)(to_above.wait_send)
-        pl.when(has_prev)(to_below.wait_send)
-    store.wait()
+        for copy in pitch[n]:
+            copy.wait_send()
+    for above, below in span + edges:
+        pl.when(has_next)(above.wait_send)
+        pl.when(has_prev)(below.wait_send)
+
+
+def store_kernel(rows_ref, out_hbm, sem):
+    copy = pltpu.make_async_copy(rows_ref.at[pl.ds(0, 1250)], out_hbm.reshape(1250, 128), sem)
+    copy.start()
+    copy.wait()
 
 
 def solution(mesh):
@@ -365,34 +483,49 @@
         rows = jnp.transpose(wake, (0, 1, 3, 4, 2)).reshape(25, 2, 5)
         out = pl.pallas_call(
             functools.partial(kernel, np_, ns_),
-            out_shape=jax.ShapeDtypeStruct((625, 2, 128), F32),
+            out_shape=jax.ShapeDtypeStruct((ROWS, 128), F32),
             in_specs=[
                 pl.BlockSpec(memory_space=pltpu.SMEM),
                 pl.BlockSpec(memory_space=pl.ANY),
                 pl.BlockSpec(memory_space=pltpu.VMEM),
             ],
-            out_specs=pl.BlockSpec(memory_space=pl.ANY),
-            scratch_shapes=[pltpu.VMEM((ROWS, 128), F32)] * 4
+            out_specs=pl.BlockSpec(memory_space=pltpu.VMEM),
+            scratch_shapes=[pltpu.VMEM((ROWS, 128), F32)] * 8
             + [
                 pltpu.VMEM((25, 2, 128), F32),
                 pltpu.VMEM((2, 128), F32),
                 pltpu.VMEM((3, 2, 128), F32),
-                pltpu.VMEM((3, 100, 128), F32),
-                pltpu.VMEM((3, 125, 128), F32),
-                pltpu.VMEM((3, 200, 128), F32),
-                pltpu.VMEM((3, 200, 128), F32),
-                pltpu.VMEM((3, 100, 128), F32),
-                pltpu.VMEM((3, 125, 128), F32),
-                pltpu.VMEM((3, 200, 128), F32),
-                pltpu.VMEM((3, 200, 128), F32),
+                pltpu.VMEM((3, 112, 128), F32),
+                pltpu.VMEM((3, 136, 128), F32),
+                pltpu.VMEM((3, 208, 128), F32),
+                pltpu.VMEM((3, 208, 128), F32),
+                pltpu.VMEM((3, 112, 128), F32),
+                pltpu.VMEM((3, 136, 128), F32),
+                pltpu.VMEM((3, 208, 128), F32),
+                pltpu.VMEM((3, 208, 128), F32),
+                pltpu.VMEM((112, 128), F32),
+                pltpu.VMEM((136, 128), F32),
+                pltpu.VMEM((2, 48, 128), F32),
+                pltpu.VMEM((2, 48, 128), F32),
+                pltpu.VMEM((2, 48, 128), F32),
+                pltpu.VMEM((2, 48, 128), F32),
                 pltpu.SemaphoreType.DMA((3, 4)),
                 pltpu.SemaphoreType.DMA((3, 4)),
+                pltpu.SemaphoreType.DMA((2, 2)),
+                pltpu.SemaphoreType.DMA((2, 2)),
                 pltpu.SemaphoreType.DMA((3,)),
                 pltpu.SemaphoreType.DMA((3,)),
                 pltpu.SemaphoreType.DMA((2,)),
             ],
             compiler_params=pltpu.CompilerParams(collective_id=0, has_side_effects=True),
         )(offsets, flat, rows)
+        out = pl.pallas_call(
+            store_kernel,
+            out_shape=jax.ShapeDtypeStruct((625, 2, 128), F32),
+            in_specs=[pl.BlockSpec(memory_space=pltpu.VMEM)],
+            out_specs=pl.BlockSpec(memory_space=pl.ANY),
+            scratch_shapes=[pltpu.SemaphoreType.DMA],
+        )(out)
         return out.reshape(state.shape)
 
     spec = P(None, None, None, None, "pitch", "span", None)

time: 43 us -> 42.7 us (level)
  local copies, waits for them, and re-layouts: 2.35 us -> 0 us
  Pallas kernels: 40.4 us -> 42.5 us
    unnamed x1 -> x0, local copies, waits for them, and re-layouts: 2.35 us -> none
    pallas_call x0 -> x1, Pallas kernels: none -> 1.95 us  [step(): pl.pallas_call(store_kernel, out_shape=jax.ShapeDtypeStruct((625, 2, 128)...]
where the time goes in v1:
time: 42.7 us; the launch traced here: 42.5 us
  Pallas kernels  42.5 us (100%)
    pallas_call x1, Pallas kernels, step(): pl.pallas_call(functools.partial(kernel, np_, ns_), out_shape=jax.ShapeDt...  40.5 us
    pallas_call x1, Pallas kernels, step(): pl.pallas_call(store_kernel, out_shape=jax.ShapeDtypeStruct((625, 2, 128)...  1.95 us

profile of v1, /device:TPU:6, one launch (start us, length us, event | category | flops | bytes accessed | tf_op | source)
XLA Modules:
  0.0 42.5 jit_solution(6817538480167959324)
XLA Ops:
  0.0 40.5 %shard_map.37.rows_ref = f32[1408,128]{1,0:T(8,128)} custom-call(s32[3]{0:T(128)} %offs_ref.1, f32[625,2,128]{2,1,0:T(2,128)} %bitcast.7, f32[25,2,5]{2,1,0:T(2,128)} %bitcast.8), custom_call_target="tpu_custom_call" | custom-call | tf_op jit(solution)/shard_map/pallas_call | solution.py:484
  40.5 1.9 %shard_map.38 = f32[625,2,128]{2,1,0:T(2,128)} custom-call(f32[1408,128]{1,0:T(8,128)} %shard_map.37.rows_ref), custom_call_target="tpu_custom_call" | custom-call | tf_op jit(solution)/shard_map/pallas_call | solution.py:522
